TPU v7x, 512 devices: a whole 4x4x16 slice. The times are simulated.
512 devices in a mesh: dp: 32 (over y_lo, z), gx: 2 (over core), gy: 8 (over x, y_hi).
Axes of the slice: x: 4, y: 4 (y_hi: 2, y_lo: 2; y = y_hi * 2 + y_lo), z: 16, core: 2. Of those that a mesh axis runs over, the one named last changes fastest.
Arguments:
- field: float32 [32, 64, 1024], P('dp', 'gx', 'gy'), may hold values from -6 to 6
- cotangent: float32 [32, 64, 1024], P('dp', 'gx', 'gy')
- checker: int32 [64, 1024], P('gx', 'gy'), may hold values from 0 to 1, as said below
- weight_in: float32 [3, 3, 32], replicated, may hold values from -2 to 2
- weight_mid: bfloat16 [3, 3, 32, 32], replicated, may hold values from -0.375 to 0.375
- weight_head: bfloat16 [2, 32], replicated, may hold values from -1 to 1
- prior_grads: float32 [32, 2, 8, 23, 9568], P('dp', 'gx', 'gy')
Outputs:
- coupled: float32 [32, 64, 1024], P('dp', 'gx', 'gy')
- field_grad: float32 [32, 64, 1024], P('dp', 'gx', 'gy')
- summed_grads: float32 [24, 9568], replicated
Inputs may be any that keep to these rules, and one draw needn't show every extreme that they name: Each row alternates along the columns: checker[i, j] = (j + p[i]) mod 2, with a parity p[i] of its own for every row i.
All inputs are finite; a program needn't handle non-finite values.
Results may differ from a plain program's by a relative error of at most 0.0034.
Values may be sent and summed in bfloat16 or wider, within the bound.
A program may use at most 64 MiB of HBM per device.

v0:
```python
import math
import jax
import jax.numpy as jnp
from jax import lax
from jax.sharding import PartitionSpec as P


def extended(value, sides, width):
    for axis, dim in sides:
        size, length = (lax.axis_size(axis), value.shape[dim])
        up = [(i, (i + 1) % size) for i in range(size)]
        down = [(j, i) for i, j in up]
        last = lax.slice_in_dim(value, length - width, length, axis=dim)
        initial = lax.slice_in_dim(value, 0, width, axis=dim)
        before = lax.ppermute(last, axis, up)
        after = lax.ppermute(initial, axis, down)
        value = jnp.concatenate([before, value, after], axis=dim)
    return value


def first_conv(padded, weight_in, row_count, col_count):
    total = jnp.zeros((weight_in.shape[2], row_count, col_count), jnp.float32)
    for row_tap in range(3):
        for col_tap in range(3):
            window = padded[row_tap : row_tap + row_count, col_tap : col_tap + col_count]
            total = total + weight_in[row_tap, col_tap][:, None, None] * window[None]
    return total


def on_device(field, cotangent, checker, weight_in, weight_mid, weight_head, prior_grads):
    highest = lax.Precision.HIGHEST
    row_count = field.shape[1]
    col_count = field.shape[2]
    hidden_width = weight_mid.shape[2]
    cell_total = (
        lax.axis_size("dp") * row_count * lax.axis_size("gx") * col_count * lax.axis_size("gy")
    )
    grad_scale = 1.0 / math.sqrt(cell_total)
    values = field[0]
    downstream = cotangent[0]
    frozen = checker.astype(jnp.float32)
    unfrozen = 1.0 - frozen
    masked = frozen * values
    partial_prior = prior_grads.reshape(prior_grads.shape[3], prior_grads.shape[4])
    padded_field = extended(masked, (("gx", 0), ("gy", 1)), 1)
    hidden_one = jnp.tanh(first_conv(padded_field, weight_in, row_count, col_count)).astype(
        jnp.bfloat16
    )
    hidden_pad = extended(hidden_one, (("gx", 1), ("gy", 2)), 1)
    hidden_inner = hidden_pad[:, 1:-1, 1:-1]
    pre_two = jnp.zeros((hidden_width, row_count, col_count), jnp.float32)
    for row_tap in range(3):
        for col_tap in range(3):
            window = hidden_pad[:, row_tap : row_tap + row_count, col_tap : col_tap + col_count]
            pre_two = pre_two + jnp.einsum(
                "oc,cxy->oxy",
                weight_mid[row_tap, col_tap],
                window,
                preferred_element_type=jnp.float32,
            )
    hidden_two = jnp.tanh(pre_two).astype(jnp.bfloat16)
    pair = jnp.einsum("ko,oxy->kxy", weight_head, hidden_two, preferred_element_type=jnp.float32)
    expo = jnp.exp(pair[0])
    coupled = masked + unfrozen * (values * expo + pair[1])
    d_pair = jnp.stack([unfrozen * downstream * values * expo, unfrozen * downstream]).astype(
        jnp.bfloat16
    )
    grad_head = jnp.einsum("kxy,oxy->ko", d_pair, hidden_two, preferred_element_type=jnp.float32)
    d_hidden_two = jnp.einsum(
        "ko,kxy->oxy", weight_head, d_pair, preferred_element_type=jnp.float32
    )
    two_f = hidden_two.astype(jnp.float32)
    d_pre_two = (d_hidden_two * (1.0 - two_f * two_f)).astype(jnp.bfloat16)
    d_two_pad = extended(d_pre_two, (("gx", 1), ("gy", 2)), 1)
    mid_list = []
    d_hidden_one = jnp.zeros((hidden_width, row_count, col_count), jnp.float32)
    for row_tap in range(3):
        for col_tap in range(3):
            window = hidden_pad[:, row_tap : row_tap + row_count, col_tap : col_tap + col_count]
            mid_list.append(
                jnp.einsum("oxy,cxy->oc", d_pre_two, window, preferred_element_type=jnp.float32)
            )
            back_window = d_two_pad[
                :, 2 - row_tap : 2 - row_tap + row_count, 2 - col_tap : 2 - col_tap + col_count
            ]
            d_hidden_one = d_hidden_one + jnp.einsum(
                "oc,oxy->cxy",
                weight_mid[row_tap, col_tap],
                back_window,
                preferred_element_type=jnp.float32,
            )
    one_f = hidden_inner.astype(jnp.float32)
    d_pre_one = d_hidden_one * (1.0 - one_f * one_f)
    in_list = []
    for row_tap in range(3):
        for col_tap in range(3):
            window = padded_field[row_tap : row_tap + row_count, col_tap : col_tap + col_count]
            in_list.append(jnp.einsum("oxy,xy->o", d_pre_one, window, precision=highest))
    d_one_pad = extended(d_pre_one, (("gx", 1), ("gy", 2)), 1)
    d_masked = jnp.zeros((row_count, col_count), jnp.float32)
    for row_tap in range(3):
        for col_tap in range(3):
            back_window = d_one_pad[
                :, 2 - row_tap : 2 - row_tap + row_count, 2 - col_tap : 2 - col_tap + col_count
            ]
            d_masked = d_masked + jnp.einsum(
                "o,oxy->xy", weight_in[row_tap, col_tap], back_window, precision=highest
            )
    field_grad = frozen * downstream + unfrozen * downstream * expo + frozen * d_masked
    layer_grads = (
        jnp.concatenate(
            [jnp.stack(in_list).reshape(-1), jnp.stack(mid_list).reshape(-1), grad_head.reshape(-1)]
        )
        * grad_scale
    )
    stacked = jnp.concatenate([layer_grads[None], partial_prior], axis=0)
    summed_grads = lax.psum(stacked, ("dp", "gx", "gy"))
    return (coupled[None], field_grad[None], summed_grads)


def solution(mesh):
    placed = (
        P("dp", "gx", "gy"),
        P("dp", "gx", "gy"),
        P("gx", "gy"),
        P(),
        P(),
        P(),
        P("dp", "gx", "gy", None, None),
    )
    return jax.shard_map(
        on_device,
        mesh=mesh,
        in_specs=placed,
        out_specs=(P("dp", "gx", "gy"), P("dp", "gx", "gy"), P()),
        check_vma=False,
    )
```

profile of v0, /device:TPU:1, one launch (start us, length us, event | category | flops | bytes accessed | tf_op | source)
XLA Modules:
  0.0 572.6 jit_solution(7181842597088774773)
XLA Ops:
  7.2 0.7 bitcast_multiply_fusion.6
  8.0 8.8 %collective-permute-start = (f32[1,128]{1,0:T(1,128)S(1)}, f32[1,128]{1,0:T(1,128)S(1)}, u32[]{:S(2)}, u32[]{:S(2)}) collective-permute-start(f32[1,128]{1,0:T(1,128)S(1)} %get-tuple-element.38), channel_id=1, source_target_pairs={{0,8},{8,0},{1,9},{9,1},{2,10},{10,2},{3,11},{11,3},{4,12},{12,4},... | collective-permute-start | bytes 1544 | tf_op jit(solution)/shard_map/ppermute | solution.py:15
  16.8 1.9 collective-permute-start.1
  18.7 0.8 slice_bitcast_fusion.8
  19.6 1.3 copy.81
  20.9 1.9 collective-permute-start.2
  22.9 7.0 %collective-permute-start.3 = (f32[34,1]{1,0:T(8,128)S(1)}, f32[34,1]{1,0:T(8,128)S(1)}, u32[]{:S(2)}, u32[]{:S(2)}) collective-permute-start(f32[34,1]{1,0:T(8,128)S(1)} %get-tuple-element.33), channel_id=1, source_target_pairs={{1,0},{2,1},{3,2},{4,3},{5,4},{6,5},{7,6},{0,7},{9,8},{10,9},{11,1... | collective-permute-start | bytes 416 | tf_op jit(solution)/shard_map/ppermute | solution.py:16
  29.9 0.9 collective-permute-done.3
  31.3 3.5 collective-permute-start.4
  34.9 1.9 collective-permute-start.5
  37.0 0.9 collective-permute-done.5
  38.1 1.9 collective-permute-start.6
  40.0 7.5 %collective-permute-start.7 = (bf16[32,34,1]{2,0,1:T(8,128)(2,1)S(1)}, bf16[32,34,1]{2,0,1:T(8,128)(2,1)S(1)}, u32[]{:S(2)}, u32[]{:S(2)}) collective-permute-start(bf16[32,34,1]{2,0,1:T(8,128)(2,1)S(1)} %get-tuple-element.16), channel_id=1, source_target_pairs={{1,0},{2,1},{3,2},{4,3},{5,4},{6,5},{7,6},{0,7},{9,8},{10,9},{11,1... | collective-permute-start | bytes 6536 | tf_op jit(solution)/shard_map/ppermute | solution.py:16
  48.0 4.6 collective-permute-done.6
  52.7 4.9 collective-permute-done.7
  60.0 0.6 fusion.96
  63.3 2.9 collective-permute-start.9
  66.1 1.9 collective-permute-start.8
  68.5 0.7 collective-permute-done.8
  69.4 5.6 collective-permute-start.10
  75.0 1.9 collective-permute-start.11
  77.5 3.5 collective-permute-done.10
  81.0 7.4 %collective-permute-done.11 = bf16[32,34,1]{2,0,1:T(8,128)(2,1)S(1)} collective-permute-done((bf16[32,34,1]{2,0,1:T(8,128)(2,1)S(1)}, bf16[32,34,1]{2,0,1:T(8,128)(2,1)S(1)}, u32[]{:S(2)}, u32[]{:S(2)}) %collective-permute-start.11) | collective-permute-done | bytes 2208 | tf_op jit(solution)/shard_map/ppermute | solution.py:15
  95.8 3.2 collective-permute-start.13
  99.0 1.9 collective-permute-start.12
  100.9 1.0 pad_maximum_fusion.1
  103.1 6.0 %collective-permute-start.14 = (f32[32,34,1]{1,0,2:T(8,128)S(1)}, f32[32,34,1]{1,0,2:T(8,128)S(1)}, u32[]{:S(2)}, u32[]{:S(2)}) collective-permute-start(f32[32,34,1]{1,0,2:T(8,128)S(1)} %copy.33), channel_id=1, source_target_pairs={{1,0},{2,1},{3,2},{4,3},{5,4},{6,5},{7,6},{0,7},{9,8},{10,9},{11,1... | collective-permute-start | bytes 13064 | tf_op jit(solution)/shard_map/ppermute | solution.py:16
  109.5 1.9 collective-permute-start.15
  112.8 4.7 collective-permute-done.15
  121.3 0.6 fusion.86
  121.9 441.7 %all-reduce.2.cloned.1.call-done = f32[24,9568]{1,0:T(8,128)} async-done(((f32[24,9568]{1,0:T(8,128)}), f32[24,9568]{1,0:T(8,128)}) %all-reduce.2.cloned.1.call-update) | async-done | bytes 918544 | tf_op jit(solution)/shard_map/psum | solution.py:117
  563.6 2.2 copy.91
  (101 shorter events, 21.6 us)
Async XLA Ops:
  7.2 52.4 %copy-start = (bf16[2,32]{1,0:T(2,128)(2,1)S(1)}, bf16[2,32]{1,0:T(2,128)(2,1)}, u32[]{:S(2)}) copy-start(bf16[2,32]{1,0:T(2,128)(2,1)} %param.12) | copy-start | bytes 388
  7.2 556.4 %all-reduce.2.cloned.1.call-start = ((), (), s32[]{:S(2)}) async-start(), calls=%async_computation | async-start | bytes 1843200 | tf_op jit(solution)/shard_map/psum | solution.py:117
  8.0 12.9 %collective-permute-start = (f32[1,128]{1,0:T(1,128)S(1)}, f32[1,128]{1,0:T(1,128)S(1)}, u32[]{:S(2)}, u32[]{:S(2)}) collective-permute-start(f32[1,128]{1,0:T(1,128)S(1)} %get-tuple-element.38), channel_id=1, source_target_pairs={{0,8},{8,0},{1,9},{9,1},{2,10},{10,2},{3,11},{11,3},{4,12},{12,4},... | collective-permute-start | bytes 1544 | tf_op jit(solution)/shard_map/ppermute | solution.py:15
  16.8 4.1 collective-permute-start.1
  19.5 17.2 %copy-start.1 = (bf16[3,3,32,32]{3,2,1,0:T(8,128)(2,1)S(1)}, bf16[3,3,32,32]{3,2,1,0:T(8,128)(2,1)}, u32[]{:S(2)}) copy-start(bf16[3,3,32,32]{3,2,1,0:T(8,128)(2,1)} %param.11) | copy-start | bytes 55300
  20.9 8.9 %collective-permute-start.2 = (f32[34,1]{1,0:T(8,128)S(1)}, f32[34,1]{1,0:T(8,128)S(1)}, u32[]{:S(2)}, u32[]{:S(2)}) collective-permute-start(f32[34,1]{1,0:T(8,128)S(1)} %get-tuple-element.32), channel_id=1, source_target_pairs={{0,1},{1,2},{2,3},{3,4},{4,5},{5,6},{6,7},{7,0},{8,9},{9,10},{10,1... | collective-permute-start | bytes 416 | tf_op jit(solution)/shard_map/ppermute | solution.py:15
  22.9 7.9 %collective-permute-start.3 = (f32[34,1]{1,0:T(8,128)S(1)}, f32[34,1]{1,0:T(8,128)S(1)}, u32[]{:S(2)}, u32[]{:S(2)}) collective-permute-start(f32[34,1]{1,0:T(8,128)S(1)} %get-tuple-element.33), channel_id=1, source_target_pairs={{1,0},{2,1},{3,2},{4,3},{5,4},{6,5},{7,6},{0,7},{9,8},{10,9},{11,1... | collective-permute-start | bytes 416 | tf_op jit(solution)/shard_map/ppermute | solution.py:16
  31.3 5.7 collective-permute-start.4
  34.9 3.1 collective-permute-start.5
  38.1 14.5 %collective-permute-start.6 = (bf16[32,34,1]{2,0,1:T(8,128)(2,1)S(1)}, bf16[32,34,1]{2,0,1:T(8,128)(2,1)S(1)}, u32[]{:S(2)}, u32[]{:S(2)}) collective-permute-start(bf16[32,34,1]{2,0,1:T(8,128)(2,1)S(1)} %get-tuple-element.15), channel_id=1, source_target_pairs={{0,1},{1,2},{2,3},{3,4},{4,5},{5,6},{6,7},{7,0},{8,9},{9,10},{10,1... | collective-permute-start | bytes 6536 | tf_op jit(solution)/shard_map/ppermute | solution.py:15
  40.0 17.5 %collective-permute-start.7 = (bf16[32,34,1]{2,0,1:T(8,128)(2,1)S(1)}, bf16[32,34,1]{2,0,1:T(8,128)(2,1)S(1)}, u32[]{:S(2)}, u32[]{:S(2)}) collective-permute-start(bf16[32,34,1]{2,0,1:T(8,128)(2,1)S(1)} %get-tuple-element.16), channel_id=1, source_target_pairs={{1,0},{2,1},{3,2},{4,3},{5,4},{6,5},{7,6},{0,7},{9,8},{10,9},{11,1... | collective-permute-start | bytes 6536 | tf_op jit(solution)/shard_map/ppermute | solution.py:16
  59.2 0.7 copy-start.2
  59.2 0.7 copy-start.4
  59.2 0.7 copy-start.5
  63.3 5.2 collective-permute-start.9
  66.1 3.1 collective-permute-start.8
  69.4 11.6 %collective-permute-start.10 = (bf16[32,34,1]{2,0,1:T(8,128)(2,1)S(1)}, bf16[32,34,1]{2,0,1:T(8,128)(2,1)S(1)}, u32[]{:S(2)}, u32[]{:S(2)}) collective-permute-start(bf16[32,34,1]{2,0,1:T(8,128)(2,1)S(1)} %get-tuple-element.11), channel_id=1, source_target_pairs={{1,0},{2,1},{3,2},{4,3},{5,4},{6,5},{7,6},{0,7},{9,8},{10,9},{11,1... | collective-permute-start | bytes 6536 | tf_op jit(solution)/shard_map/ppermute | solution.py:16
  75.0 13.3 %collective-permute-start.11 = (bf16[32,34,1]{2,0,1:T(8,128)(2,1)S(1)}, bf16[32,34,1]{2,0,1:T(8,128)(2,1)S(1)}, u32[]{:S(2)}, u32[]{:S(2)}) collective-permute-start(bf16[32,34,1]{2,0,1:T(8,128)(2,1)S(1)} %get-tuple-element.12), channel_id=1, source_target_pairs={{0,1},{1,2},{2,3},{3,4},{4,5},{5,6},{6,7},{7,0},{8,9},{9,10},{10,1... | collective-permute-start | bytes 6536 | tf_op jit(solution)/shard_map/ppermute | solution.py:15
  95.4 6.6 %copy-start.3 = (f32[3,3,32]{2,1,0:T(4,128)S(1)}, f32[3,3,32]{2,1,0:T(4,128)}, u32[]{:S(2)}) copy-start(f32[3,3,32]{2,1,0:T(4,128)} %param.10) | copy-start | bytes 3460
  95.8 6.6 %collective-permute-start.13 = (f32[32,1,128]{2,0,1:T(8,128)S(1)}, f32[32,1,128]{2,0,1:T(8,128)S(1)}, u32[]{:S(2)}, u32[]{:S(2)}) collective-permute-start(f32[32,1,128]{2,0,1:T(8,128)S(1)} %get-tuple-element.8), channel_id=1, source_target_pairs={{8,0},{0,8},{9,1},{1,9},{10,2},{2,10},{11,3},{3,11},{12,4},{4,12},... | collective-permute-start | bytes 49160 | tf_op jit(solution)/shard_map/ppermute | solution.py:16
  99.0 3.4 collective-permute-start.12
  103.1 9.1 %collective-permute-start.14 = (f32[32,34,1]{1,0,2:T(8,128)S(1)}, f32[32,34,1]{1,0,2:T(8,128)S(1)}, u32[]{:S(2)}, u32[]{:S(2)}) collective-permute-start(f32[32,34,1]{1,0,2:T(8,128)S(1)} %copy.33), channel_id=1, source_target_pairs={{1,0},{2,1},{3,2},{4,3},{5,4},{6,5},{7,6},{0,7},{9,8},{10,9},{11,1... | collective-permute-start | bytes 13064 | tf_op jit(solution)/shard_map/ppermute | solution.py:16
  109.5 8.1 %collective-permute-start.15 = (f32[32,34,1]{1,0,2:T(8,128)S(1)}, f32[32,34,1]{1,0,2:T(8,128)S(1)}, u32[]{:S(2)}, u32[]{:S(2)}) collective-permute-start(f32[32,34,1]{1,0,2:T(8,128)S(1)} %copy.35), channel_id=1, source_target_pairs={{0,1},{1,2},{2,3},{3,4},{4,5},{5,6},{6,7},{7,0},{8,9},{9,10},{10,1... | collective-permute-start | bytes 13064 | tf_op jit(solution)/shard_map/ppermute | solution.py:15
Sparse Core Ops, SparseCore 0:
  102.5 461.0 all-reduce.1
where the time goes:
time: 573 us
  waiting for transfers between devices  469 us (82%)
  starting transfers between devices  59.9 us (10%)
  matrix products  16.1 us (3%)
  between operations  14.6 us (3%)
  local copies, waits for them, and re-layouts  7.8 us (1%)
    psum x1, waiting for transfers between devices, on_device(): summed_grads = lax.psum(stacked, ('dp', 'gx', 'gy'))  442 us
    ppermute x8, starting transfers between devices, extended(): after = lax.ppermute(initial, axis, down)  36 us
    ppermute x8, starting transfers between devices, extended(): before = lax.ppermute(last, axis, up)  23.8 us
    ppermute x8, waiting for transfers between devices, extended(): before = lax.ppermute(last, axis, up)  17.5 us
  transfers between devices with their start and end apart: 17, of which 9 were waited for; matrix products, arithmetic and copies ran while one was open for 2% of the time, Pallas kernels for 0%

commit v1 on v0

--- a/solution.py
+++ b/solution.py
@@ -114,7 +114,7 @@
         * grad_scale
     )
     stacked = jnp.concatenate([layer_grads[None], partial_prior], axis=0)
-    summed_grads = lax.psum(stacked, ("dp", "gx", "gy"))
+    summed_grads = lax.psum(lax.psum(stacked, "dp"), ("gx", "gy"))
     return (coupled[None], field_grad[None], summed_grads)
 
 

time: 573 us -> 527 us (0.920)
  waiting for transfers between devices: 469 us -> 422 us
    psum x1 -> x2, waiting for transfers between devices: 442 us -> 394 us  [on_device(): summed_grads = lax.psum(lax.psum(stacked, 'dp'), ('gx', 'gy'))]
  transfers between devices with their start and end apart: 17 -> 18, of which waited for: 9 -> 10; matrix products, arithmetic and copies ran while one was open for 2% -> 3% of each run, Pallas kernels for 0% -> 0%
where the time goes in v1:
time: 527 us
  waiting for transfers between devices  422 us (80%)
  starting transfers between devices  59.9 us (11%)
  matrix products  16.2 us (3%)
  between operations  14.6 us (3%)
  local copies, waits for them, and re-layouts  8.54 us (2%)
  other arithmetic  5.95 us (1%)
    psum x2, waiting for transfers between devices, on_device(): summed_grads = lax.psum(lax.psum(stacked, 'dp'), ('gx', 'gy'))  394 us
    ppermute x8, starting transfers between devices, extended(): after = lax.ppermute(initial, axis, down)  35.8 us
    ppermute x8, starting transfers between devices, extended(): before = lax.ppermute(last, axis, up)  23.8 us
    ppermute x8, waiting for transfers between devices, extended(): before = lax.ppermute(last, axis, up)  17.5 us
  transfers between devices with their start and end apart: 18, of which 10 were waited for; matrix products, arithmetic and copies ran while one was open for 3% of the time, Pallas kernels for 0%

profile of v1, /device:TPU:1, one launch (start us, length us, event | category | flops | bytes accessed | tf_op | source)
XLA Modules:
  0.0 526.7 jit_solution(14420198657777059344)
XLA Ops:
  7.2 0.7 bitcast_multiply_fusion.6
  8.0 8.8 %collective-permute-start = (f32[1,128]{1,0:T(1,128)S(1)}, f32[1,128]{1,0:T(1,128)S(1)}, u32[]{:S(2)}, u32[]{:S(2)}) collective-permute-start(f32[1,128]{1,0:T(1,128)S(1)} %get-tuple-element.38), channel_id=1, source_target_pairs={{0,8},{8,0},{1,9},{9,1},{2,10},{10,2},{3,11},{11,3},{4,12},{12,4},... | collective-permute-start | bytes 1544 | tf_op jit(solution)/shard_map/ppermute | solution.py:15
  16.8 1.9 collective-permute-start.1
  18.7 0.8 slice_bitcast_fusion.8
  19.6 1.3 copy.81
  20.9 1.9 collective-permute-start.2
  22.9 7.0 %collective-permute-start.3 = (f32[34,1]{1,0:T(8,128)S(1)}, f32[34,1]{1,0:T(8,128)S(1)}, u32[]{:S(2)}, u32[]{:S(2)}) collective-permute-start(f32[34,1]{1,0:T(8,128)S(1)} %get-tuple-element.33), channel_id=1, source_target_pairs={{1,0},{2,1},{3,2},{4,3},{5,4},{6,5},{7,6},{0,7},{9,8},{10,9},{11,1... | collective-permute-start | bytes 416 | tf_op jit(solution)/shard_map/ppermute | solution.py:16
  29.9 0.9 collective-permute-done.3
  31.3 3.5 collective-permute-start.4
  34.9 1.9 collective-permute-start.5
  37.0 0.9 collective-permute-done.5
  38.1 1.9 collective-permute-start.6
  40.0 7.5 %collective-permute-start.7 = (bf16[32,34,1]{2,0,1:T(8,128)(2,1)S(1)}, bf16[32,34,1]{2,0,1:T(8,128)(2,1)S(1)}, u32[]{:S(2)}, u32[]{:S(2)}) collective-permute-start(bf16[32,34,1]{2,0,1:T(8,128)(2,1)S(1)} %get-tuple-element.16), channel_id=1, source_target_pairs={{1,0},{2,1},{3,2},{4,3},{5,4},{6,5},{7,6},{0,7},{9,8},{10,9},{11,1... | collective-permute-start | bytes 6536 | tf_op jit(solution)/shard_map/ppermute | solution.py:16
  48.0 4.6 collective-permute-done.6
  52.7 4.9 collective-permute-done.7
  63.3 2.9 collective-permute-start.9
  66.2 1.9 collective-permute-start.8
  69.4 5.6 %collective-permute-start.10 = (bf16[32,34,1]{2,0,1:T(8,128)(2,1)S(1)}, bf16[32,34,1]{2,0,1:T(8,128)(2,1)S(1)}, u32[]{:S(2)}, u32[]{:S(2)}) collective-permute-start(bf16[32,34,1]{2,0,1:T(8,128)(2,1)S(1)} %get-tuple-element.11), channel_id=1, source_target_pairs={{1,0},{2,1},{3,2},{4,3},{5,4},{6,5},{7,6},{0,7},{9,8},{10,9},{11,1... | collective-permute-start | bytes 6536 | tf_op jit(solution)/shard_map/ppermute | solution.py:16
  75.0 1.9 collective-permute-start.11
  77.5 3.5 collective-permute-done.10
  81.0 7.4 %collective-permute-done.11 = bf16[32,34,1]{2,0,1:T(8,128)(2,1)S(1)} collective-permute-done((bf16[32,34,1]{2,0,1:T(8,128)(2,1)S(1)}, bf16[32,34,1]{2,0,1:T(8,128)(2,1)S(1)}, u32[]{:S(2)}, u32[]{:S(2)}) %collective-permute-start.11) | collective-permute-done | bytes 2208 | tf_op jit(solution)/shard_map/ppermute | solution.py:15
  95.8 3.2 collective-permute-start.13
  99.0 1.9 collective-permute-start.12
  100.9 1.0 pad_maximum_fusion.1
  103.3 5.8 %collective-permute-start.14 = (f32[32,34,1]{1,0,2:T(8,128)S(1)}, f32[32,34,1]{1,0,2:T(8,128)S(1)}, u32[]{:S(2)}, u32[]{:S(2)}) collective-permute-start(f32[32,34,1]{1,0,2:T(8,128)S(1)} %copy.33), channel_id=1, source_target_pairs={{1,0},{2,1},{3,2},{4,3},{5,4},{6,5},{7,6},{0,7},{9,8},{10,9},{11,1... | collective-permute-start | bytes 13064 | tf_op jit(solution)/shard_map/ppermute | solution.py:16
  109.5 1.9 collective-permute-start.15
  112.9 4.7 collective-permute-done.15
  117.6 1.4 copy.36
  119.0 1.4 pad_maximum_fusion
  121.8 214.8 %all-reduce.3.cloned.1.call-done = f32[24,9568]{1,0:T(8,128)} async-done(((f32[24,9568]{1,0:T(8,128)}), f32[24,9568]{1,0:T(8,128)}) %all-reduce.3.cloned.1.call-update) | async-done | bytes 918544 | tf_op jit(solution)/shard_map/psum | solution.py:117
  338.5 179.1 %all-reduce.5.cloned.1.call-done = f32[24,9568]{1,0:T(8,128)} async-done(((f32[24,9568]{1,0:T(8,128)}), f32[24,9568]{1,0:T(8,128)}) %all-reduce.5.cloned.1.call-update) | async-done | bytes 918544 | tf_op jit(solution)/shard_map/psum | solution.py:117
  517.7 2.2 copy.92
  (104 shorter events, 22.8 us)
Async XLA Ops:
  7.2 52.4 %copy-start = (bf16[2,32]{1,0:T(2,128)(2,1)S(1)}, bf16[2,32]{1,0:T(2,128)(2,1)}, u32[]{:S(2)}) copy-start(bf16[2,32]{1,0:T(2,128)(2,1)} %param.12) | copy-start | bytes 388
  7.2 329.4 %all-reduce.3.cloned.1.call-start = ((), (), s32[]{:S(2)}) async-start(), calls=%async_computation | async-start | bytes 1843200 | tf_op jit(solution)/shard_map/psum | solution.py:117
  8.0 12.9 %collective-permute-start = (f32[1,128]{1,0:T(1,128)S(1)}, f32[1,128]{1,0:T(1,128)S(1)}, u32[]{:S(2)}, u32[]{:S(2)}) collective-permute-start(f32[1,128]{1,0:T(1,128)S(1)} %get-tuple-element.38), channel_id=1, source_target_pairs={{0,8},{8,0},{1,9},{9,1},{2,10},{10,2},{3,11},{11,3},{4,12},{12,4},... | collective-permute-start | bytes 1544 | tf_op jit(solution)/shard_map/ppermute | solution.py:15
  16.8 4.1 collective-permute-start.1
  19.5 17.2 %copy-start.1 = (bf16[3,3,32,32]{3,2,1,0:T(8,128)(2,1)S(1)}, bf16[3,3,32,32]{3,2,1,0:T(8,128)(2,1)}, u32[]{:S(2)}) copy-start(bf16[3,3,32,32]{3,2,1,0:T(8,128)(2,1)} %param.11) | copy-start | bytes 55300
  20.9 8.9 %collective-permute-start.2 = (f32[34,1]{1,0:T(8,128)S(1)}, f32[34,1]{1,0:T(8,128)S(1)}, u32[]{:S(2)}, u32[]{:S(2)}) collective-permute-start(f32[34,1]{1,0:T(8,128)S(1)} %get-tuple-element.32), channel_id=1, source_target_pairs={{0,1},{1,2},{2,3},{3,4},{4,5},{5,6},{6,7},{7,0},{8,9},{9,10},{10,1... | collective-permute-start | bytes 416 | tf_op jit(solution)/shard_map/ppermute | solution.py:15
  22.9 7.9 %collective-permute-start.3 = (f32[34,1]{1,0:T(8,128)S(1)}, f32[34,1]{1,0:T(8,128)S(1)}, u32[]{:S(2)}, u32[]{:S(2)}) collective-permute-start(f32[34,1]{1,0:T(8,128)S(1)} %get-tuple-element.33), channel_id=1, source_target_pairs={{1,0},{2,1},{3,2},{4,3},{5,4},{6,5},{7,6},{0,7},{9,8},{10,9},{11,1... | collective-permute-start | bytes 416 | tf_op jit(solution)/shard_map/ppermute | solution.py:16
  31.3 5.7 %collective-permute-start.4 = (bf16[32,1,128]{2,0,1:T(8,128)(2,1)S(1)}, bf16[32,1,128]{2,0,1:T(8,128)(2,1)S(1)}, u32[]{:S(2)}, u32[]{:S(2)}) collective-permute-start(bf16[32,1,128]{2,0,1:T(8,128)(2,1)S(1)} %get-tuple-element.19), channel_id=1, source_target_pairs={{0,8},{8,0},{1,9},{9,1},{2,10},{10,2},{3,11},{11,3},{4,12},{12,4},... | collective-permute-start | bytes 24584 | tf_op jit(solution)/shard_map/ppermute | solution.py:15
  34.9 3.1 collective-permute-start.5
  38.1 14.5 %collective-permute-start.6 = (bf16[32,34,1]{2,0,1:T(8,128)(2,1)S(1)}, bf16[32,34,1]{2,0,1:T(8,128)(2,1)S(1)}, u32[]{:S(2)}, u32[]{:S(2)}) collective-permute-start(bf16[32,34,1]{2,0,1:T(8,128)(2,1)S(1)} %get-tuple-element.15), channel_id=1, source_target_pairs={{0,1},{1,2},{2,3},{3,4},{4,5},{5,6},{6,7},{7,0},{8,9},{9,10},{10,1... | collective-permute-start | bytes 6536 | tf_op jit(solution)/shard_map/ppermute | solution.py:15
  40.0 17.5 %collective-permute-start.7 = (bf16[32,34,1]{2,0,1:T(8,128)(2,1)S(1)}, bf16[32,34,1]{2,0,1:T(8,128)(2,1)S(1)}, u32[]{:S(2)}, u32[]{:S(2)}) collective-permute-start(bf16[32,34,1]{2,0,1:T(8,128)(2,1)S(1)} %get-tuple-element.16), channel_id=1, source_target_pairs={{1,0},{2,1},{3,2},{4,3},{5,4},{6,5},{7,6},{0,7},{9,8},{10,9},{11,1... | collective-permute-start | bytes 6536 | tf_op jit(solution)/shard_map/ppermute | solution.py:16
  59.2 0.7 copy-start.2
  59.2 0.7 copy-start.4
  59.2 0.7 copy-start.5
  63.3 5.2 collective-permute-start.9
  66.2 3.1 collective-permute-start.8
  69.4 11.5 %collective-permute-start.10 = (bf16[32,34,1]{2,0,1:T(8,128)(2,1)S(1)}, bf16[32,34,1]{2,0,1:T(8,128)(2,1)S(1)}, u32[]{:S(2)}, u32[]{:S(2)}) collective-permute-start(bf16[32,34,1]{2,0,1:T(8,128)(2,1)S(1)} %get-tuple-element.11), channel_id=1, source_target_pairs={{1,0},{2,1},{3,2},{4,3},{5,4},{6,5},{7,6},{0,7},{9,8},{10,9},{11,1... | collective-permute-start | bytes 6536 | tf_op jit(solution)/shard_map/ppermute | solution.py:16
  75.0 13.3 %collective-permute-start.11 = (bf16[32,34,1]{2,0,1:T(8,128)(2,1)S(1)}, bf16[32,34,1]{2,0,1:T(8,128)(2,1)S(1)}, u32[]{:S(2)}, u32[]{:S(2)}) collective-permute-start(bf16[32,34,1]{2,0,1:T(8,128)(2,1)S(1)} %get-tuple-element.12), channel_id=1, source_target_pairs={{0,1},{1,2},{2,3},{3,4},{4,5},{5,6},{6,7},{7,0},{8,9},{9,10},{10,1... | collective-permute-start | bytes 6536 | tf_op jit(solution)/shard_map/ppermute | solution.py:15
  95.4 6.6 %copy-start.3 = (f32[3,3,32]{2,1,0:T(4,128)S(1)}, f32[3,3,32]{2,1,0:T(4,128)}, u32[]{:S(2)}) copy-start(f32[3,3,32]{2,1,0:T(4,128)} %param.10) | copy-start | bytes 3460
  95.8 6.8 %collective-permute-start.13 = (f32[32,1,128]{2,0,1:T(8,128)S(1)}, f32[32,1,128]{2,0,1:T(8,128)S(1)}, u32[]{:S(2)}, u32[]{:S(2)}) collective-permute-start(f32[32,1,128]{2,0,1:T(8,128)S(1)} %get-tuple-element.8), channel_id=1, source_target_pairs={{8,0},{0,8},{9,1},{1,9},{10,2},{2,10},{11,3},{3,11},{12,4},{4,12},... | collective-permute-start | bytes 49160 | tf_op jit(solution)/shard_map/ppermute | solution.py:16
  99.0 3.6 collective-permute-start.12
  102.4 415.3 %all-reduce.5.cloned.1.call-start = ((), (), s32[]{:S(2)}) async-start(), calls=%async_computation.1 | async-start | bytes 1843200 | tf_op jit(solution)/shard_map/psum | solution.py:117
  103.3 8.9 %collective-permute-start.14 = (f32[32,34,1]{1,0,2:T(8,128)S(1)}, f32[32,34,1]{1,0,2:T(8,128)S(1)}, u32[]{:S(2)}, u32[]{:S(2)}) collective-permute-start(f32[32,34,1]{1,0,2:T(8,128)S(1)} %copy.33), channel_id=1, source_target_pairs={{1,0},{2,1},{3,2},{4,3},{5,4},{6,5},{7,6},{0,7},{9,8},{10,9},{11,1... | collective-permute-start | bytes 13064 | tf_op jit(solution)/shard_map/ppermute | solution.py:16
  109.5 8.1 %collective-permute-start.15 = (f32[32,34,1]{1,0,2:T(8,128)S(1)}, f32[32,34,1]{1,0,2:T(8,128)S(1)}, u32[]{:S(2)}, u32[]{:S(2)}) collective-permute-start(f32[32,34,1]{1,0,2:T(8,128)S(1)} %copy.35), channel_id=1, source_target_pairs={{0,1},{1,2},{2,3},{3,4},{4,5},{5,6},{6,7},{7,0},{8,9},{9,10},{10,1... | collective-permute-start | bytes 13064 | tf_op jit(solution)/shard_map/ppermute | solution.py:15
Sparse Core Ops, SparseCore 0:
  102.5 234.0 all-reduce.2
  339.8 177.8 all-reduce.4
